TPU v7x, 256 devices: a whole 4x4x8 slice. The times are simulated.
256 devices in a mesh: gx: 64 (over x, z, core), af: 4 (over y).
Axes of the slice: x: 4, y: 4, z: 8, core: 2. Of those that a mesh axis runs over, the one named last changes fastest.
Arguments:
- scalar_field: float32 [128, 512, 512], P('gx', 'af'), may hold values from -256 to 256
- plane_sketch: float32 [128, 2, 256], P('gx'), may hold values from -0.5 to 0.5
- second_sketch: float32 [512, 256], P('af'), may hold values from -0.25 to 0.25
- third_sketch: float32 [512, 256], replicated, may hold values from -0.25 to 0.25
- mixing: float32 [2, 256, 128], replicated, may hold values from -0.375 to 0.375
- plane_targets: int32 [128, 2], replicated, may hold values from 0 to 7
- plane_signs: int32 [128, 2], replicated, may hold values from 0 to 1
Outputs:
- factor_second: float32 [512, 128], P(('af', 'gx'))
- factor_third: float32 [512, 128], P(('gx', 'af'))
- core_sketch: float32 [128, 128, 128], P('gx', 'af')
Inputs may be any that keep to these rules, and one draw needn't show every extreme that they name: `plane_targets`: block id of each of a plane's two entries in the core sketch; the two may coincide. `plane_signs`: 1 stands for a plus sign, 0 for a minus sign.
All inputs are finite; a program needn't handle non-finite values.
Results may differ from a plain program's by a relative error of at most 0.0003.
Values sent between devices are 32-bit elements; how exact they have to be, the bound alone decides.
A program may use at most 64 MiB of HBM per device.

v0:
```python
import jax
import jax.numpy as jnp
from jax import lax
from jax.sharding import PartitionSpec as P

BLOCK = 16
BLOCKS = 8
precise = lax.Precision.HIGHEST


def gram_of(ranged):
    return jnp.dot(ranged.T, ranged, precision=precise)


def orthonormal_rows(ranged, gram_matrix):
    lower_factor = jnp.linalg.cholesky(gram_matrix)
    return jax.scipy.linalg.solve_triangular(lower_factor, ranged.T, lower=True).T


def selector(targets, sign_values, row_count):
    row_ids = jnp.arange(row_count, dtype=jnp.int32)
    return jnp.sum(
        jnp.where(targets[None, :, :] == row_ids[:, None, None], sign_values[None, :, :], 0.0),
        axis=2,
    )


def body(
    scalar_field, plane_sketch, second_sketch, third_sketch, mixing, plane_targets, plane_signs
):
    planes, rows, cells = scalar_field.shape
    rank_cols = mixing.shape[2]
    gx_index = lax.axis_index("gx")
    af_index = lax.axis_index("af")
    gx_size = lax.axis_size("gx")
    af_size = lax.axis_size("af")
    along_second = jnp.einsum("pjl,lk->pjk", scalar_field, third_sketch, precision=precise)
    partial_second = jnp.einsum(
        "pjk,pk->jk", along_second, plane_sketch[:, 0, :], precision=precise
    )
    along_third = jnp.einsum("pjl,jk->plk", scalar_field, second_sketch, precision=precise)
    partial_third = jnp.einsum("plk,pk->lk", along_third, plane_sketch[:, 1, :], precision=precise)
    range_second_block = jnp.dot(partial_second, mixing[0], precision=precise)
    range_third = jnp.dot(partial_third, mixing[1], precision=precise)
    full_rows = rows * af_size
    range_second = lax.dynamic_update_slice_in_dim(
        jnp.zeros((full_rows, rank_cols), jnp.float32), range_second_block, af_index * rows, 0
    )
    both = lax.psum(jnp.stack([range_second, range_third]), ("gx", "af"))
    rows_second, rows_third = (both[0], both[1])
    factor_second_all = orthonormal_rows(rows_second, gram_of(rows_second))
    factor_third_all = orthonormal_rows(rows_third, gram_of(rows_third))
    out_second = full_rows // (gx_size * af_size)
    factor_second = lax.dynamic_slice_in_dim(
        factor_second_all, (af_index * gx_size + gx_index) * out_second, out_second, 0
    )
    factor_third = lax.dynamic_slice_in_dim(
        factor_third_all, (gx_index * af_size + af_index) * out_second, out_second, 0
    )
    basis_second = lax.dynamic_slice_in_dim(factor_second_all, af_index * rows, rows, 0)
    left_side = jnp.einsum("jr,pjl->prl", basis_second, scalar_field, precision=precise)
    projected = jnp.einsum("prl,ls->prs", left_side, factor_third_all, precision=precise)
    out_rows = BLOCKS * BLOCK // gx_size
    plane_ids = jnp.arange(plane_targets.shape[0], dtype=jnp.int32)
    all_targets = plane_targets * BLOCK + (plane_ids % BLOCK)[:, None]
    all_signs = (2 * plane_signs - 1).astype(jnp.float32)
    first_plane = gx_index * planes
    own_targets = lax.dynamic_slice_in_dim(all_targets, first_plane, planes, 0)
    own_signs = lax.dynamic_slice_in_dim(all_signs, first_plane, planes, 0)
    flattened = projected.reshape(planes, -1)
    select = selector(own_targets, own_signs, gx_size * out_rows)
    partial_core = lax.psum_scatter(
        jnp.dot(select, flattened, precision=precise).reshape(
            gx_size * out_rows, rank_cols, rank_cols
        ),
        "gx",
        scatter_dimension=0,
        tiled=True,
    )
    core_sketch = lax.psum_scatter(partial_core, "af", scatter_dimension=1, tiled=True)
    return (factor_second, factor_third, core_sketch)


def solution(mesh):
    in_specs = (P("gx", "af", None), P("gx", None, None), P("af", None), P(), P(), P(), P())
    out_specs = (P(("af", "gx"), None), P(("gx", "af"), None), P("gx", "af", None))
    return jax.shard_map(body, mesh=mesh, in_specs=in_specs, out_specs=out_specs, check_vma=False)
```

profile of v0, /device:TPU:2, one launch (start us, length us, event | category | flops | bytes accessed | tf_op | source)
XLA Modules:
  0.0 544.3 jit_solution(9497696338969925887)
XLA Ops:
  7.2 0.0 all-reduce.4.cloned.1.call-start
  7.2 0.8 fusion.37
  8.0 0.2 copy-done
  8.2 2.0 fusion.1
  10.2 1.5 convolution_bitcast_fusion.2
  11.7 1.6 fusion.3
  13.4 1.2 fusion.4
  14.6 0.8 pad_maximum_fusion
  15.4 0.2 reduce-scatter.2.cloned.1.call-start
  15.7 0.7 add_convert_fusion
  16.4 0.7 multiply_add_fusion
  17.1 0.1 constant_dynamic-slice_fusion
  17.1 0.1 copy.38
  17.2 0.1 constant_dynamic-slice_fusion.1
  17.3 0.1 copy.37
  17.4 0.1 fusion.34
  17.5 253.1 %all-reduce.4.cloned.1.call-done = f32[2,512,128]{2,1,0:T(8,128)} async-done(((f32[2,512,128]{2,1,0:T(8,128)}), f32[2,512,128]{2,1,0:T(8,128)}) %all-reduce.4.cloned.1.call-update) | async-done | bytes 524304 | tf_op jit(solution)/shard_map/psum | solution.py:49
  270.6 1.6 fusion.13
  272.2 0.1 copy.35
  272.3 11.7 %cholesky.44 = f32[128,128]{1,0:T(8,128)S(1)} custom-call(f32[128,128]{1,0:T(8,128)S(1)} %fusion.32), custom_call_target="Cholesky" | custom-call | tf_op jit(solution)/shard_map/jit(cholesky)/cholesky | solution.py:16
  284.0 0.6 compare_reduce_fusion.1
  284.7 0.7 fusion.26
  285.4 9.8 %custom-call.6 = f32[1,128,128]{1,2,0:T(8,128)S(1)} custom-call(f32[1,128,128]{2,1,0:T(8,128)S(1)} %fusion.26), custom_call_target="InvertDiagBlocksLowerTriangular" | custom-call | tf_op jit(solution)/shard_map/jit(_solve_triangular)/triangular_solve | solution.py:17
  295.2 1.6 fusion.11
  296.8 0.1 copy.36
  296.9 11.7 %cholesky.55 = f32[128,128]{1,0:T(8,128)S(1)} custom-call(f32[128,128]{1,0:T(8,128)S(1)} %fusion.30), custom_call_target="Cholesky" | custom-call | tf_op jit(solution)/shard_map/jit(cholesky)/cholesky | solution.py:16
  308.7 0.6 compare_reduce_fusion
  309.3 0.7 fusion.27
  310.0 10.0 %custom-call.7 = f32[1,128,128]{1,2,0:T(8,128)S(1)} custom-call(f32[1,128,128]{2,1,0:T(8,128)S(1)} %fusion.27), custom_call_target="InvertDiagBlocksLowerTriangular" | custom-call | tf_op jit(solution)/shard_map/jit(_solve_triangular)/triangular_solve | solution.py:17
  320.0 1.4 fusion.8
  321.3 0.6 convolution_bitcast_fusion.1
  321.9 1.4 fusion.6
  323.3 0.6 convolution_bitcast_fusion.4
  323.9 6.8 %fusion.19 = f32[128,128,128]{2,0,1:T(8,128)S(1)} fusion(f32[1,2,128,128]{3,2,1,0:T(8,128)S(1)} %convolution_bitcast_fusion.4, f32[128,2]{0,1:T(2,128)S(1)} %fusion.34), kind=kOutput, calls=%fused_computation.27 | convolution fusion | flops 50331648 | bytes 8520704 | tf_op jit(solution)/shard_map/dot_general | solution.py:73
  330.7 8.3 %copy.39 = f32[128,128,128]{2,1,0:T(8,128)} copy(f32[128,128,128]{2,0,1:T(8,128)S(1)} %fusion.19) | data formatting | bytes 16777216 | tf_op jit(solution)/shard_map/dot_general | solution.py:73
  339.0 0.0 reduce-scatter.2.cloned.1.call-update
  339.0 0.0 all-reduce.6.cloned.1.call-start
  339.1 0.6 copy-done.1
  339.7 0.6 dynamic-slice.12
  340.9 147.6 %reduce-scatter.2.cloned.1.call-done = f32[2,128,128]{2,1,0:T(8,128)} async-done(((f32[128,128,128]{2,1,0:T(8,128)}), f32[2,128,128]{2,1,0:T(8,128)}) %reduce-scatter.2.cloned.1.call-update) | async-done | bytes 131088 | tf_op jit(solution)/shard_map/reduce_scatter | solution.py:72
  488.6 1.6 copy.40
  490.2 0.1 dynamic-slice_bitcast_fusion.1
  490.3 0.6 copy.41
  490.9 0.1 dynamic-slice_bitcast_fusion
  491.0 0.6 copy.42
  491.7 44.7 %all-reduce.6.cloned.1.call-done = f32[2,128,128]{2,0,1:T(2,128)} async-done(((f32[2,128,128]{2,0,1:T(2,128)}), f32[2,128,128]{2,0,1:T(2,128)}) %all-reduce.6.cloned.1.call-update) | async-done | bytes 131088
  536.4 0.8 constant_dynamic-slice_fusion.2
  537.1 0.6 copy.43
  (11 shorter events, 0.2 us)
Async XLA Ops:
  7.2 1.1 copy-start
  7.2 263.4 %all-reduce.4.cloned.1.call-start = ((), (), s32[]{:S(2)}) async-start(), calls=%async_computation.1 | async-start | bytes 1048576 | tf_op jit(solution)/shard_map/psum | solution.py:49
  15.4 473.1 %reduce-scatter.2.cloned.1.call-start = ((), (), s32[]{:S(2)}) async-start(), calls=%async_computation.2 | async-start | bytes 8519680 | tf_op jit(solution)/shard_map/reduce_scatter | solution.py:72
  339.0 0.7 copy-start.1
  339.0 197.4 %all-reduce.6.cloned.1.call-start = ((), (), s32[]{:S(2)}) async-start(), calls=%async_computation.3 | async-start | bytes 262144
Sparse Core Ops, SparseCore 0:
  15.6 254.9 all-reduce.3
  339.1 149.3 reduce-scatter.1
  491.0 45.3 all-reduce.5
where the time goes:
time: 545 us; the launch traced here: 544 us
  waiting for transfers between devices  445 us (82%)
  other arithmetic  48.2 us (9%)
  matrix products  20.2 us (4%)
  local copies, waits for them, and re-layouts  15.5 us (3%)
  between operations  14.6 us (3%)
    psum x1, waiting for transfers between devices, body(): both = lax.psum(jnp.stack([range_second, range_third]), ('gx', 'af'))  253 us
    reduce_scatter x1, waiting for transfers between devices, body(): lax.psum_scatter(jnp.dot(select, flattened, precision=precise).reshape(gx...  148 us
    unnamed x4, waiting for transfers between devices  44.8 us
    another operation x6, other arithmetic, orthonormal_rows(): lower_factor = jnp.linalg.cholesky(gram_matrix)  24.8 us
    another operation x4, other arithmetic, orthonormal_rows(): jax.scipy.linalg.solve_triangular(lower_factor, ranged.T, lower=True)  21.1 us
  transfers between devices with their start and end apart: 3, of which 3 were waited for; matrix products, arithmetic and copies ran while one was open for 1% of the time, Pallas kernels for 0%

commit v1 on v0

--- a/solution.py
+++ b/solution.py
@@ -2,6 +2,7 @@
 import jax.numpy as jnp
 from jax import lax
 from jax.sharding import PartitionSpec as P
+from jax.lax import psum
 
 BLOCK = 16
 BLOCKS = 8
@@ -46,7 +47,8 @@
     range_second = lax.dynamic_update_slice_in_dim(
         jnp.zeros((full_rows, rank_cols), jnp.float32), range_second_block, af_index * rows, 0
     )
-    both = lax.psum(jnp.stack([range_second, range_third]), ("gx", "af"))
+    field = jnp.stack([range_second, range_third])
+    both = psum(psum(field, "gx"), "af")
     rows_second, rows_third = (both[0], both[1])
     factor_second_all = orthonormal_rows(rows_second, gram_of(rows_second))
     factor_third_all = orthonormal_rows(rows_third, gram_of(rows_third))

time: 545 us -> 524 us (0.961)
  waiting for transfers between devices: 445 us -> 424 us
    psum x1 -> x2, waiting for transfers between devices: 253 us -> 230 us  [body(): both = psum(psum(field, 'gx'), 'af')]
    unnamed x4 -> x5, waiting for transfers between devices: 44.8 us -> 44.7 us
  transfers between devices with their start and end apart: 3 -> 4, of which waited for: 3 -> 4; matrix products, arithmetic and copies ran while one was open for 1% -> 1% of each run, Pallas kernels for 0% -> 0%
where the time goes in v1:
time: 524 us; the launch traced here: 523 us
  waiting for transfers between devices  424 us (81%)
  other arithmetic  48.2 us (9%)
  matrix products  20.2 us (4%)
  local copies, waits for them, and re-layouts  15.5 us (3%)
  between operations  14.6 us (3%)
    psum x2, waiting for transfers between devices, body(): both = psum(psum(field, 'gx'), 'af')  230 us
    reduce_scatter x1, waiting for transfers between devices, body(): lax.psum_scatter(jnp.dot(select, flattened, precision=precise).reshape(gx...  149 us
    unnamed x5, waiting for transfers between devices  44.7 us
    another operation x6, other arithmetic, orthonormal_rows(): lower_factor = jnp.linalg.cholesky(gram_matrix)  24.8 us
    another operation x4, other arithmetic, orthonormal_rows(): jax.scipy.linalg.solve_triangular(lower_factor, ranged.T, lower=True)  21.1 us
  transfers between devices with their start and end apart: 4, of which 4 were waited for; matrix products, arithmetic and copies ran while one was open for 1% of the time, Pallas kernels for 0%

profile of v1, /device:TPU:2, one launch (start us, length us, event | category | flops | bytes accessed | tf_op | source)
XLA Modules:
  0.0 523.2 jit_solution(12720356529253345325)
XLA Ops:
  7.2 0.8 fusion.37
  8.0 0.2 copy-done
  8.2 2.0 fusion.1
  10.2 1.5 convolution_bitcast_fusion.2
  11.7 1.6 fusion.3
  13.4 1.2 fusion.4
  14.6 0.8 pad_maximum_fusion
  15.4 0.0 all-reduce.7.cloned.1.call-start
  15.5 0.7 add_convert_fusion
  16.2 0.1 constant_dynamic-slice_fusion
  16.3 0.1 copy.38
  16.4 183.5 %all-reduce.5.cloned.1.call-done = f32[2,512,128]{2,1,0:T(8,128)} async-done(((f32[2,512,128]{2,1,0:T(8,128)}), f32[2,512,128]{2,1,0:T(8,128)}) %all-reduce.5.cloned.1.call-update) | async-done | bytes 524304 | tf_op jit(solution)/shard_map/psum | solution.py:51
  199.9 0.2 reduce-scatter.2.cloned.1.call-start
  200.1 0.7 multiply_add_fusion
  200.8 0.1 constant_dynamic-slice_fusion.1
  200.9 0.1 copy.37
  201.0 0.1 fusion.34
  201.1 46.8 %all-reduce.7.cloned.1.call-done = f32[2,512,128]{2,1,0:T(8,128)} async-done(((f32[2,512,128]{2,1,0:T(8,128)}), f32[2,512,128]{2,1,0:T(8,128)}) %all-reduce.7.cloned.1.call-update) | async-done | bytes 524304 | tf_op jit(solution)/shard_map/psum | solution.py:51
  247.9 1.6 fusion.13
  249.5 0.1 copy.35
  249.6 11.7 %cholesky.44 = f32[128,128]{1,0:T(8,128)S(1)} custom-call(f32[128,128]{1,0:T(8,128)S(1)} %fusion.32), custom_call_target="Cholesky" | custom-call | tf_op jit(solution)/shard_map/jit(cholesky)/cholesky | solution.py:17
  261.4 0.6 compare_reduce_fusion.1
  262.0 0.7 fusion.26
  262.7 9.8 %custom-call.6 = f32[1,128,128]{1,2,0:T(8,128)S(1)} custom-call(f32[1,128,128]{2,1,0:T(8,128)S(1)} %fusion.26), custom_call_target="InvertDiagBlocksLowerTriangular" | custom-call | tf_op jit(solution)/shard_map/jit(_solve_triangular)/triangular_solve | solution.py:18
  272.5 1.6 fusion.11
  274.1 0.1 copy.36
  274.2 11.7 %cholesky.55 = f32[128,128]{1,0:T(8,128)S(1)} custom-call(f32[128,128]{1,0:T(8,128)S(1)} %fusion.30), custom_call_target="Cholesky" | custom-call | tf_op jit(solution)/shard_map/jit(cholesky)/cholesky | solution.py:17
  286.0 0.6 compare_reduce_fusion
  286.6 0.7 fusion.27
  287.3 10.0 %custom-call.7 = f32[1,128,128]{1,2,0:T(8,128)S(1)} custom-call(f32[1,128,128]{2,1,0:T(8,128)S(1)} %fusion.27), custom_call_target="InvertDiagBlocksLowerTriangular" | custom-call | tf_op jit(solution)/shard_map/jit(_solve_triangular)/triangular_solve | solution.py:18
  297.3 1.4 fusion.8
  298.7 0.6 convolution_bitcast_fusion.1
  299.3 1.4 fusion.6
  300.6 0.6 convolution_bitcast_fusion.4
  301.2 6.8 %fusion.19 = f32[128,128,128]{2,0,1:T(8,128)S(1)} fusion(f32[1,2,128,128]{3,2,1,0:T(8,128)S(1)} %convolution_bitcast_fusion.4, f32[128,2]{0,1:T(2,128)S(1)} %fusion.34), kind=kOutput, calls=%fused_computation.27 | convolution fusion | flops 50331648 | bytes 8520704 | tf_op jit(solution)/shard_map/dot_general | solution.py:75
  308.0 8.3 %copy.39 = f32[128,128,128]{2,1,0:T(8,128)} copy(f32[128,128,128]{2,0,1:T(8,128)S(1)} %fusion.19) | data formatting | bytes 16777216 | tf_op jit(solution)/shard_map/dot_general | solution.py:75
  316.4 0.0 all-reduce.9.cloned.1.call-start
  316.4 0.6 copy-done.1
  317.0 0.6 dynamic-slice.12
  318.2 149.3 %reduce-scatter.2.cloned.1.call-done = f32[2,128,128]{2,1,0:T(8,128)} async-done(((f32[128,128,128]{2,1,0:T(8,128)}), f32[2,128,128]{2,1,0:T(8,128)}) %reduce-scatter.2.cloned.1.call-update) | async-done | bytes 131088 | tf_op jit(solution)/shard_map/reduce_scatter | solution.py:74
  467.5 1.6 copy.40
  469.2 0.1 dynamic-slice_bitcast_fusion.1
  469.3 0.6 copy.41
  469.9 0.1 dynamic-slice_bitcast_fusion
  470.0 0.6 copy.42
  470.6 44.6 %all-reduce.9.cloned.1.call-done = f32[2,128,128]{2,0,1:T(2,128)} async-done(((f32[2,128,128]{2,0,1:T(2,128)}), f32[2,128,128]{2,0,1:T(2,128)}) %all-reduce.9.cloned.1.call-update) | async-done | bytes 131088
  515.2 0.8 constant_dynamic-slice_fusion.2
  516.0 0.6 copy.43
  (14 shorter events, 0.2 us)
Async XLA Ops:
  7.2 1.1 copy-start
  7.2 192.7 %all-reduce.5.cloned.1.call-start = ((), (), s32[]{:S(2)}) async-start(), calls=%async_computation.1 | async-start | bytes 1048576 | tf_op jit(solution)/shard_map/psum | solution.py:51
  15.4 232.5 %all-reduce.7.cloned.1.call-start = ((), (), s32[]{:S(2)}) async-start(), calls=%async_computation.2 | async-start | bytes 1048576 | tf_op jit(solution)/shard_map/psum | solution.py:51
  199.9 267.6 %reduce-scatter.2.cloned.1.call-start = ((), (), s32[]{:S(2)}) async-start(), calls=%async_computation.3 | async-start | bytes 8519680 | tf_op jit(solution)/shard_map/reduce_scatter | solution.py:74
  316.3 0.7 copy-start.1
  316.4 198.9 %all-reduce.9.cloned.1.call-start = ((), (), s32[]{:S(2)}) async-start(), calls=%async_computation.4 | async-start | bytes 262144
Sparse Core Ops, SparseCore 0:
  15.6 184.2 all-reduce.4
  202.2 45.6 all-reduce.6
  316.5 150.9 reduce-scatter.1
  469.8 45.4 all-reduce.8
